TPU v7x, 32 devices: a whole 2x2x4 slice. The times are simulated.
32 devices in a mesh: dp: 4 (over y, x), expert: 8 (over z, core).
Axes of the slice: x: 2, y: 2, z: 4, core: 2. Of those that a mesh axis runs over, the one named last changes fastest.
Arguments:
- tokens: bfloat16 [4096, 2048], P(('dp', 'expert')), may hold values from -6 to 6
- out_grad: bfloat16 [4096, 2048], P(('dp', 'expert')), may hold values from -6 to 6
- routes: int32 [4096, 3], P(('dp', 'expert')), may hold values from 0 to 7, all different within a row; in each aligned block of 128 rows (0 to 127, 128 to 255, ...) at most 64 rows name the same one
- probs: bfloat16 [4096, 3], P(('dp', 'expert')), may hold values from 0.099609375 to 1
- w_in: bfloat16 [8, 2048, 1536], P('expert'), may hold values from -0.125 to 0.125
- w_out: bfloat16 [8, 768, 2048], P('expert'), may hold values from -0.21875 to 0.21875
Outputs:
- token_grad: bfloat16 [4096, 2048], P(('dp', 'expert'))
- prob_grad: bfloat16 [4096, 3], P(('dp', 'expert'))
- w_in_grad: bfloat16 [8, 2048, 1536], P('expert', 'dp')
- w_out_grad: bfloat16 [8, 768, 2048], P('expert', None, 'dp')
Inputs may be any that keep to these rules, and one draw needn't show every extreme that they name: `routes`: each row names 3 different experts. In each device's aligned block of 128 rows no expert is named more than 64 times, a bound that some block reaches.
All inputs are finite; a program needn't handle non-finite values.
Results may differ from a plain program's by a relative error of at most 0.014.
Values may be sent and summed in bfloat16 or wider, within the bound.
A program may use at most 128 MiB of HBM per device.

v0:
```python
import jax
import jax.numpy as jnp
from jax import lax
from jax.sharding import PartitionSpec as P


def silu_parts(gate):
    sig = jax.nn.sigmoid(gate)
    return (gate * sig, sig * (1.0 + gate * (1.0 - sig)))


def shards(tokens, out_grad, routes, probs, w_in, w_out):
    tok_rows, width = tokens.shape
    top_count = routes.shape[1]
    n_groups = lax.axis_size("expert")
    experts = n_groups * w_in.shape[0]
    hidden = w_out.shape[1]
    cap = 4 * tok_rows * top_count // (3 * experts)
    flat = routes.reshape(-1)
    assigned = flat.shape[0]
    hits = (flat[:, None] == jnp.arange(experts, dtype=jnp.int32)[None, :]).astype(jnp.int32)
    rank = jnp.sum((jnp.cumsum(hits, axis=0) - hits) * hits, axis=1)
    slot = flat * cap + rank
    slot_hit = slot[:, None] == jnp.arange(experts * cap, dtype=jnp.int32)[None, :]
    filled = jnp.any(slot_hit, axis=0)
    owner = jnp.sum(jnp.where(slot_hit, jnp.arange(assigned, dtype=jnp.int32)[:, None], 0), axis=0)
    source = owner // top_count
    zero_b = jnp.zeros((), jnp.bfloat16)
    send_x = jnp.where(filled[:, None], tokens[source], zero_b).reshape(experts, cap, width)
    send_dy = jnp.where(filled[:, None], out_grad[source], zero_b).reshape(experts, cap, width)
    send_p = jnp.where(filled, probs.reshape(-1)[owner], zero_b).reshape(experts, cap)
    recv_x, recv_dy, recv_p = (
        lax.all_to_all(send_x, "expert", split_axis=0, concat_axis=0, tiled=True),
        lax.all_to_all(send_dy, "expert", split_axis=0, concat_axis=0, tiled=True),
        lax.all_to_all(send_p, "expert", split_axis=0, concat_axis=0, tiled=True),
    )
    rows_x = recv_x.reshape(-1, width)
    rows_dy = recv_dy.reshape(-1, width)
    rows_p = recv_p.reshape(-1)
    w_one = w_in[0]
    w_two = w_out[0]
    proj = jnp.dot(rows_x, w_one, preferred_element_type=jnp.float32)
    gate, upper = (proj[:, :hidden], proj[:, hidden:])
    act, slope = silu_parts(gate)
    hid = (act * upper).astype(jnp.bfloat16)
    outs = jnp.dot(hid, w_two, preferred_element_type=jnp.float32).astype(jnp.bfloat16)
    slot_grad = (rows_p.astype(jnp.float32)[:, None] * rows_dy.astype(jnp.float32)).astype(
        jnp.bfloat16
    )
    hid_grad = jnp.dot(slot_grad, w_two.T, preferred_element_type=jnp.float32)
    proj_grad = jnp.concatenate([hid_grad * upper * slope, hid_grad * act], axis=1).astype(
        jnp.bfloat16
    )
    row_grad = jnp.dot(proj_grad, w_one.T, preferred_element_type=jnp.float32).astype(jnp.bfloat16)
    dprob = jnp.sum(rows_dy.astype(jnp.float32) * outs.astype(jnp.float32), axis=1).astype(
        jnp.bfloat16
    )
    back_x, back_p = (
        lax.all_to_all(
            row_grad.reshape(n_groups, cap, width),
            "expert",
            split_axis=0,
            concat_axis=0,
            tiled=True,
        ),
        lax.all_to_all(
            dprob.reshape(n_groups, cap), "expert", split_axis=0, concat_axis=0, tiled=True
        ),
    )
    prob_grad = back_p.reshape(-1)[slot].reshape(tok_rows, top_count)
    picked = back_x.reshape(experts * cap, width)[slot].astype(jnp.float32)
    token_grad = jnp.sum(picked.reshape(tok_rows, top_count, width), axis=1).astype(jnp.bfloat16)
    contract = (((0,), (0,)), ((), ()))
    grad_one = lax.dot_general(rows_x, proj_grad, contract, preferred_element_type=jnp.float32)
    grad_two = lax.dot_general(hid, slot_grad, contract, preferred_element_type=jnp.float32)
    share_one, share_two = (
        lax.psum_scatter(
            grad_one.astype(jnp.bfloat16), "dp", scatter_dimension=0, tiled=True
        ).astype(jnp.float32),
        lax.psum_scatter(
            grad_two.astype(jnp.bfloat16), "dp", scatter_dimension=1, tiled=True
        ).astype(jnp.float32),
    )
    w_in_grad = share_one.astype(jnp.bfloat16)[None]
    w_out_grad = share_two.astype(jnp.bfloat16)[None]
    return (token_grad, prob_grad, w_in_grad, w_out_grad)


def solution(mesh):
    return jax.shard_map(
        shards,
        mesh=mesh,
        in_specs=(
            P(("dp", "expert"), None),
            P(("dp", "expert"), None),
            P(("dp", "expert"), None),
            P(("dp", "expert"), None),
            P("expert", None, None),
            P("expert", None, None),
        ),
        out_specs=(
            P(("dp", "expert"), None),
            P(("dp", "expert"), None),
            P("expert", "dp", None),
            P("expert", None, "dp"),
        ),
        check_vma=False,
    )
```

profile of v0, /device:TPU:0, one launch (start us, length us, event | category | flops | bytes accessed | tf_op | source)
XLA Modules:
  0.0 282.2 jit_solution(2178853500060580334)
XLA Ops:
  7.2 0.9 copy.28
  8.5 0.9 reduce-window.6
  10.2 0.8 copy.30
  11.2 3.5 %gather_fusion = bf16[512]{0:T(512)(128)(2,1)S(1)} fusion(bf16[384]{0:T(512)(128)(2,1)S(1)} %reshape.208, s32[1024]{0:T(1024)S(1)} %pad_clamp_fusion.2), kind=kCustom, calls=%fused_computation | custom fusion | bytes 4096 | tf_op jit(solution)/shard_map/gather | solution.py:31
  14.7 0.7 select_n.81
  15.4 6.4 %all-to-all-start = ((bf16[8,1,64]{2,1,0:T(2,128)(2,1)}), bf16[8,1,64]{2,1,0:T(2,128)(2,1)S(1)}, u32[]{:S(2)}, u32[]{:S(2)}) async-start(bf16[8,1,64]{2,1,0:T(2,128)(2,1)} %select_n.81), calls=%async_computation | async-start | bytes 8192 | tf_op jit(solution)/shard_map/all_to_all | solution.py:35
  21.9 6.4 %gather_fusion.2 = bf16[512,2048]{1,0:T(8,128)(2,1)} fusion(bf16[128,2048]{1,0:T(8,128)(2,1)} %param.6, s32[1024]{0:T(1024)S(1)} %pad_clamp_fusion.1), kind=kCustom, calls=%fused_computation.2 | custom fusion | bytes 4196352 | tf_op jit(solution)/shard_map/gather | solution.py:29
  28.2 6.4 %gather_fusion.1 = bf16[512,2048]{1,0:T(8,128)(2,1)} fusion(bf16[128,2048]{1,0:T(8,128)(2,1)} %param.7, s32[1024]{0:T(1024)S(1)} %pad_clamp_fusion.1), kind=kCustom, calls=%fused_computation.1 | custom fusion | bytes 4196352 | tf_op jit(solution)/shard_map/gather | solution.py:30
  34.6 4.6 %broadcast_select_fusion = (bf16[8,64,2048]{2,1,0:T(8,128)(2,1)}, bf16[8,64,2048]{2,1,0:T(8,128)(2,1)}) fusion(bf16[8,64,2048]{2,1,0:T(8,128)(2,1)} %bitcast.52, pred[8,64]{1,0:T(8,128)(4,1)S(1)} %broadcast_in_dim.55, bf16[8,64,2048]{2,1,0:T(8,128)(2,1)} %bitcast.53), kind=kLoop, calls=%fused_computation.23 | loop fusion | flops 2097152 | bytes 8389120 | tf_op jit(solution)/shard_map/jit(_where)/select_n | solution.py:29
  39.2 54.2 %all_to_all.27 = bf16[8,64,2048]{2,1,0:T(8,128)(2,1)} all-to-all(bf16[8,64,2048]{2,1,0:T(8,128)(2,1)} %get-tuple-element.25), channel_id=1, replica_groups=mesh['dp'=4,'expert'=8] {'expert'}, dimensions={0} | all-to-all | bytes 4194304 | tf_op jit(solution)/shard_map/all_to_all | solution.py:33
  93.5 4.3 %all-to-all-start.1 = ((bf16[8,64,2048]{2,1,0:T(8,128)(2,1)}), bf16[8,64,2048]{2,1,0:T(8,128)(2,1)}, u32[]{:S(2)}, u32[]{:S(2)}) async-start(bf16[8,64,2048]{2,1,0:T(8,128)(2,1)} %get-tuple-element.26), calls=%async_computation.1 | async-start | bytes 4194304 | tf_op jit(solution)/shard_map/all_to_all | solution.py:34
  98.1 8.5 %fusion.2 = f32[512,1536]{1,0:T(8,128)} fusion(bf16[512,2048]{1,0:T(8,128)(2,1)} %bitcast.55, bf16[1,2048,1536]{2,1,0:T(8,128)(2,1)} %param.10), kind=kOutput, calls=%fused_computation.8 | convolution fusion | flops 3221225472 | bytes 11534336 | tf_op jit(solution)/shard_map/dot_general | solution.py:42
  106.6 40.2 %all-to-all-done.1 = bf16[8,64,2048]{2,1,0:T(8,128)(2,1)} async-done(((bf16[8,64,2048]{2,1,0:T(8,128)(2,1)}), bf16[8,64,2048]{2,1,0:T(8,128)(2,1)}, u32[]{:S(2)}, u32[]{:S(2)}) %all-to-all-start.1) | async-done | bytes 2097184 | tf_op jit(solution)/shard_map/all_to_all | solution.py:34
  146.8 2.1 fusion.4
  149.0 0.4 copy-done.3
  149.4 3.5 %multiply_convert_fusion.2 = (bf16[512,768]{1,0:T(8,128)(2,1)}, bf16[512,768]{1,0:T(8,128)(2,1)}, bf16[512,768]{1,0:T(8,128)(2,1)S(1)}) fusion(f32[512,1536]{1,0:T(8,128)S(1)} %copy-done.3, bf16[512,2048]{1,0:T(8,128)(2,1)S(1)} %bitcast.54, bf16[1,768,2048]{2,1,0:T(8,128)(2,1)S(1)} %copy-done), kind=kOutput, calls=%fused_computation.28 | convolution fusion | flops 1616510976 | bytes 10747904 | tf_op jit(solution)/shard_map/dot_general | solution.py:50
  152.9 2.3 fusion.6
  155.2 3.6 %convolution_convert_fusion.1 = bf16[768,2048]{1,0:T(8,128)(2,1)} fusion(bf16[512,768]{1,0:T(8,128)(2,1)S(1)} %get-tuple-element.22, bf16[512,2048]{1,0:T(8,128)(2,1)S(1)} %fusion.6), kind=kOutput, calls=%fused_computation.16 | convolution fusion | flops 1612185600 | bytes 6029312 | tf_op jit(solution)/shard_map/dot_general | solution.py:75
  158.8 8.1 %convolution_convert_fusion = bf16[2048,1536]{1,0:T(8,128)(2,1)} fusion(bf16[512,2048]{1,0:T(8,128)(2,1)} %bitcast.56, bf16[512,768]{1,0:T(8,128)(2,1)} %get-tuple-element.21, bf16[512,768]{1,0:T(8,128)(2,1)} %get-tuple-element.20), kind=kOutput, calls=%fused_computation.5 | convolution fusion | flops 3227516928 | bytes 9961472 | tf_op jit(solution)/shard_map/dot_general | solution.py:74
  167.0 3.7 %fusion.5 = bf16[512]{0:T(512)(128)(2,1)S(1)} fusion(bf16[8,64,2048]{2,1,0:T(8,128)(2,1)} %all-to-all-done.1, bf16[512,768]{1,0:T(8,128)(2,1)} %copy-done.2, bf16[1,768,2048]{2,1,0:T(8,128)(2,1)S(1)} %copy-done), kind=kOutput, calls=%fused_computation.14 | convolution fusion | flops 1615855104 | bytes 6030336 | tf_op jit(solution)/shard_map/dot_general | solution.py:46
  170.7 0.7 convert_element_type.104
  171.4 3.5 %all-to-all-start.4 = ((bf16[8,1,64]{2,1,0:T(2,128)(2,1)}), bf16[8,1,64]{2,1,0:T(2,128)(2,1)S(1)}, u32[]{:S(2)}, u32[]{:S(2)}) async-start(bf16[8,1,64]{2,1,0:T(2,128)(2,1)} %convert_element_type.104), calls=%async_computation.4 | async-start | bytes 8192 | tf_op jit(solution)/shard_map/all_to_all | solution.py:66
  174.9 8.2 %fusion.14 = bf16[512,2048]{1,0:T(8,128)(2,1)} fusion(bf16[1,2048,1536]{2,1,0:T(8,128)(2,1)} %param.10, bf16[512,768]{1,0:T(8,128)(2,1)} %get-tuple-element.21, bf16[512,768]{1,0:T(8,128)(2,1)} %get-tuple-element.20), kind=kOutput, calls=%fused_computation.22 | convolution fusion | flops 3225419776 | bytes 9961472 | tf_op jit(solution)/shard_map/dot_general | solution.py:54
  183.2 4.9 %all-to-all-start.3 = ((bf16[8,64,2048]{2,1,0:T(8,128)(2,1)}), bf16[8,64,2048]{2,1,0:T(8,128)(2,1)}, u32[]{:S(2)}, u32[]{:S(2)}) async-start(bf16[8,64,2048]{2,1,0:T(8,128)(2,1)} %bitcast.57), calls=%async_computation.3 | async-start | bytes 4194304 | tf_op jit(solution)/shard_map/all_to_all | solution.py:59
  188.6 2.8 gather_fusion.4
  191.4 0.2 reshape.213
  191.6 0.7 copy.34
  192.3 45.0 %all-to-all-done.3 = bf16[8,64,2048]{2,1,0:T(8,128)(2,1)} async-done(((bf16[8,64,2048]{2,1,0:T(8,128)(2,1)}), bf16[8,64,2048]{2,1,0:T(8,128)(2,1)}, u32[]{:S(2)}, u32[]{:S(2)}) %all-to-all-start.3) | async-done | bytes 2097184 | tf_op jit(solution)/shard_map/all_to_all | solution.py:59
  237.3 6.9 %gather_fusion.3 = bf16[384,2048]{1,0:T(8,128)(2,1)} fusion(bf16[512,2048]{1,0:T(8,128)(2,1)} %bitcast.13, s32[1024]{0:T(1024)S(1)} %pad_clamp_fusion), kind=kCustom, calls=%fused_computation.3 | custom fusion | bytes 3147264 | tf_op jit(solution)/shard_map/gather | solution.py:71
  244.2 5.1 %gather.27 = bf16[128,3,2048]{2,1,0:T(4,128)(2,1)} reshape(bf16[384,2048]{1,0:T(8,128)(2,1)} %gather_fusion.3) | data formatting | bytes 3145728 | tf_op jit(solution)/shard_map/gather | solution.py:71
  249.3 5.0 %reduce_sum.47 = bf16[128,2048]{1,0:T(8,128)(2,1)} reduce(bf16[128,3,2048]{2,1,0:T(4,128)(2,1)} %gather.27, bf16[]{:T(256)} %constant.9.clone.1), dimensions={1}, to_apply=%region_5.6 | reduce | flops 524288 | bytes 2097154 | tf_op jit(solution)/shard_map/reduce_sum | solution.py:72
  254.3 21.1 %reduce-scatter.3.cloned.1.call-done = bf16[512,1536]{1,0:T(8,128)(2,1)} async-done(((bf16[2048,1536]{1,0:T(8,128)(2,1)}), bf16[512,1536]{1,0:T(8,128)(2,1)}) %reduce-scatter.3.cloned.1.call-update) | async-done | bytes 1572880 | tf_op jit(solution)/shard_map/reduce_scatter | solution.py:77
  (39 shorter events, 2.3 us)
Async XLA Ops:
  7.2 141.8 %copy-start = (bf16[1,768,2048]{2,1,0:T(8,128)(2,1)S(1)}, bf16[1,768,2048]{2,1,0:T(8,128)(2,1)}, u32[]{:S(2)}) copy-start(bf16[1,768,2048]{2,1,0:T(8,128)(2,1)} %param.11) | copy-start | bytes 9437188
  15.4 23.8 %all-to-all-start = ((bf16[8,1,64]{2,1,0:T(2,128)(2,1)}), bf16[8,1,64]{2,1,0:T(2,128)(2,1)S(1)}, u32[]{:S(2)}, u32[]{:S(2)}) async-start(bf16[8,1,64]{2,1,0:T(2,128)(2,1)} %select_n.81), calls=%async_computation | async-start | bytes 8192 | tf_op jit(solution)/shard_map/all_to_all | solution.py:35
  93.5 53.4 %all-to-all-start.1 = ((bf16[8,64,2048]{2,1,0:T(8,128)(2,1)}), bf16[8,64,2048]{2,1,0:T(8,128)(2,1)}, u32[]{:S(2)}, u32[]{:S(2)}) async-start(bf16[8,64,2048]{2,1,0:T(8,128)(2,1)} %get-tuple-element.26), calls=%async_computation.1 | async-start | bytes 4194304 | tf_op jit(solution)/shard_map/all_to_all | solution.py:34
  97.8 156.5 %reduce-scatter.5.cloned.1.call-start = ((), (), s32[]{:S(2)}) async-start(), calls=%async_computation.8 | async-start | bytes 3932160 | tf_op jit(solution)/shard_map/reduce_scatter | solution.py:80
  146.8 2.5 copy-start.3
  152.9 2.3 copy-start.2
  158.8 116.6 %reduce-scatter.3.cloned.1.call-start = ((), (), s32[]{:S(2)}) async-start(), calls=%async_computation.7 | async-start | bytes 7864320 | tf_op jit(solution)/shard_map/reduce_scatter | solution.py:77
  171.4 11.8 %all-to-all-start.4 = ((bf16[8,1,64]{2,1,0:T(2,128)(2,1)}), bf16[8,1,64]{2,1,0:T(2,128)(2,1)S(1)}, u32[]{:S(2)}, u32[]{:S(2)}) async-start(bf16[8,1,64]{2,1,0:T(2,128)(2,1)} %convert_element_type.104), calls=%async_computation.4 | async-start | bytes 8192 | tf_op jit(solution)/shard_map/all_to_all | solution.py:66
  183.2 4.9 %copy-start.1 = (s32[128,3]{0,1:T(4,128)S(1)}, s32[128,3]{0,1:T(4,128)}, u32[]{:S(2)}) copy-start(s32[128,3]{0,1:T(4,128)} %param.8) | copy-start | bytes 4612
  183.2 54.1 %all-to-all-start.3 = ((bf16[8,64,2048]{2,1,0:T(8,128)(2,1)}), bf16[8,64,2048]{2,1,0:T(8,128)(2,1)}, u32[]{:S(2)}, u32[]{:S(2)}) async-start(bf16[8,64,2048]{2,1,0:T(8,128)(2,1)} %bitcast.57), calls=%async_computation.3 | async-start | bytes 4194304 | tf_op jit(solution)/shard_map/all_to_all | solution.py:59
Sparse Core Ops, SparseCore 0:
  158.9 42.8 reduce-scatter.4
  205.3 70.0 reduce-scatter.2
where the time goes:
time: 283 us; the launch traced here: 282 us
  waiting for transfers between devices  106 us (37%)
  blocking collectives  54.2 us (19%)
  local copies, waits for them, and re-layouts  37 us (13%)
  matrix products  35.7 us (13%)
  starting transfers between devices  19.4 us (7%)
  other arithmetic  15.4 us (5%)
  between operations  14.2 us (5%)
    all_to_all x1, blocking collectives, shards(): lax.all_to_all(send_x, 'expert', split_axis=0, concat_axis=0, tiled=True)  54.2 us
    all_to_all x1, waiting for transfers between devices, shards(): lax.all_to_all(row_grad.reshape(n_groups, cap, width), 'expert', split_ax...  45 us
    all_to_all x1, waiting for transfers between devices, shards(): lax.all_to_all(send_dy, 'expert', split_axis=0, concat_axis=0, tiled=True)  40.2 us
    reduce_scatter x1, waiting for transfers between devices, shards(): lax.psum_scatter(grad_one.astype(jnp.bfloat16), 'dp', scatter_dimension=0...  21.1 us
    gather x2, local copies, waits for them, and re-layouts, shards(): picked = back_x.reshape(experts * cap, width)[slot].astype(jnp.float32)  12.1 us
    dot_general x1, matrix products, shards(): proj = jnp.dot(rows_x, w_one, preferred_element_type=jnp.float32)  8.5 us
    dot_general x1, matrix products, shards(): jnp.dot(proj_grad, w_one.T, preferred_element_type=jnp.float32)  8.25 us
    dot_general x1, matrix products, shards(): lax.dot_general(rows_x, proj_grad, contract, preferred_element_type=jnp.f...  8.13 us
  transfers between devices with their start and end apart: 6, of which 3 were waited for; matrix products, arithmetic and copies ran while one was open for 24% of the time, Pallas kernels for 0%

commit v1 on v0

v1 whole, which is shorter than its diff:
```python
import jax
import jax.numpy as jnp
from jax import lax
from jax.sharding import PartitionSpec as P

F32 = jnp.float32
BF16 = jnp.bfloat16


def exclusive_rank(hits):
    rows = hits.shape[1]
    earlier = (jnp.arange(rows)[:, None] < jnp.arange(rows)[None, :]).astype(BF16)
    return jnp.dot(hits.astype(BF16), earlier, preferred_element_type=F32)


def dispatch_gather(tokens, out_grad, routes, probs, cap):
    tok_rows, width = tokens.shape
    top = routes.shape[1]
    me = lax.axis_index("expert").astype(F32)
    table = jnp.concatenate([routes.T.astype(BF16), probs.T], axis=0)
    table = lax.all_gather(table, "expert", axis=0, tiled=False).astype(F32)
    all_x = lax.all_gather(tokens, "expert", axis=0, tiled=False)
    all_dy = lax.all_gather(out_grad, "expert", axis=0, tiled=False)
    mine = table[:, :top] == me
    hits = jnp.any(mine, axis=1)
    prob = jnp.sum(jnp.where(mine, table[:, top:], 0.0), axis=1)
    rank = exclusive_rank(hits)
    place = (rank[:, None, :] == jnp.arange(cap, dtype=F32)[None, :, None]) & hits[:, None, :]
    pick = place.astype(BF16)
    rows_p = jnp.sum(jnp.where(place, prob[:, None, :], 0.0), axis=2).reshape(-1)

    def take(rows):
        out = lax.dot_general(pick, rows, (((2,), (1,)), ((0,), (0,))), preferred_element_type=F32)
        return out.astype(BF16).reshape(-1, width)

    return take(all_x), take(all_dy), rows_p


def dispatch_exchange(tokens, out_grad, probs, slot, experts, cap):
    tok_rows, width = tokens.shape
    top = slot.shape[1]
    flat = slot.reshape(-1)
    slot_hit = flat[:, None] == jnp.arange(experts * cap, dtype=jnp.int32)[None, :]
    filled = jnp.any(slot_hit, axis=0)
    owner = jnp.sum(jnp.where(slot_hit, jnp.arange(flat.shape[0], dtype=jnp.int32)[:, None], 0), axis=0)
    source = owner // top
    zero = jnp.zeros((), BF16)

    def move(rows):
        return lax.all_to_all(rows, "expert", split_axis=0, concat_axis=0, tiled=True)

    send_x = jnp.where(filled[:, None], tokens[source], zero).reshape(experts, cap, width)
    send_dy = jnp.where(filled[:, None], out_grad[source], zero).reshape(experts, cap, width)
    send_p = jnp.where(filled, probs.reshape(-1)[owner], zero).reshape(experts, cap)
    return (
        move(send_x).reshape(-1, width),
        move(send_dy).reshape(-1, width),
        move(send_p).reshape(-1).astype(F32),
    )


def shards(tokens, out_grad, routes, probs, w_in, w_out):
    tok_rows, width = tokens.shape
    top = routes.shape[1]
    n_groups = lax.axis_size("expert")
    experts = n_groups * w_in.shape[0]
    hidden = w_out.shape[1]
    cap = 4 * tok_rows * top // (3 * experts)
    w_one, w_two = w_in[0], w_out[0]

    names = jnp.arange(experts, dtype=jnp.int32)
    named = routes[:, :, None] == names[None, None, :]
    hits = jnp.any(named, axis=1)
    later = (jnp.arange(tok_rows)[:, None] > jnp.arange(tok_rows)[None, :]).astype(BF16)
    rank = jnp.dot(later, hits.astype(BF16), preferred_element_type=F32)
    own_rank = jnp.sum(jnp.where(named, rank[:, None, :], 0.0), axis=2).astype(jnp.int32)
    slot = routes * cap + own_rank

    if experts <= 16:
        rows_x, rows_dy, rows_p = dispatch_gather(tokens, out_grad, routes, probs, cap)
    else:
        rows_x, rows_dy, rows_p = dispatch_exchange(tokens, out_grad, probs, slot, experts, cap)
    rows_p = rows_p[:, None]

    proj = jnp.dot(rows_x, w_one, preferred_element_type=F32)
    gate, upper = proj[:, :hidden], proj[:, hidden:]
    sig = jax.nn.sigmoid(gate)
    act = gate * sig
    hid = (act * upper).astype(BF16)
    scaled = (rows_p * hid.astype(F32)).astype(BF16)
    contract = (((0,), (0,)), ((), ()))
    grad_two = lax.dot_general(scaled, rows_dy, contract, preferred_element_type=F32).astype(BF16)
    share_two = lax.psum_scatter(grad_two, "dp", scatter_dimension=1, tiled=True)

    back = lax.dot_general(rows_dy, w_two, (((1,), (1,)), ((), ())), preferred_element_type=F32)
    dprob = jnp.sum(back * hid.astype(F32), axis=1).astype(BF16)
    hid_grad = rows_p * back
    proj_grad = jnp.concatenate(
        [hid_grad * upper * (sig * (1.0 + gate * (1.0 - sig))), hid_grad * act], axis=1
    ).astype(BF16)
    grad_one = lax.dot_general(rows_x, proj_grad, contract, preferred_element_type=F32).astype(BF16)
    share_one = lax.psum_scatter(grad_one, "dp", scatter_dimension=0, tiled=True)

    row_grad = lax.dot_general(
        proj_grad, w_one, (((1,), (1,)), ((), ())), preferred_element_type=F32
    ).astype(BF16)
    back_x = lax.all_to_all(
        row_grad.reshape(n_groups, cap, width), "expert", split_axis=0, concat_axis=0, tiled=True
    ).reshape(experts * cap, width)
    back_p = lax.all_to_all(
        dprob.reshape(n_groups, cap), "expert", split_axis=0, concat_axis=0, tiled=True
    ).reshape(-1)
    slots = jnp.arange(experts * cap, dtype=jnp.int32)
    held = slot[:, :, None] == slots[None, None, :]
    prob_grad = jnp.sum(jnp.where(held, back_p.astype(F32), 0.0), axis=2).astype(BF16)
    token_grad = jnp.dot(
        jnp.any(held, axis=1).astype(BF16), back_x, preferred_element_type=F32
    ).astype(BF16)
    return token_grad, prob_grad, share_one[None], share_two[None]


def solution(mesh):
    return jax.shard_map(
        shards,
        mesh=mesh,
        in_specs=(
            P(("dp", "expert"), None),
            P(("dp", "expert"), None),
            P(("dp", "expert"), None),
            P(("dp", "expert"), None),
            P("expert", None, None),
            P("expert", None, None),
        ),
        out_specs=(
            P(("dp", "expert"), None),
            P(("dp", "expert"), None),
            P("expert", "dp", None),
            P("expert", None, "dp"),
        ),
        check_vma=False,
    )
```

time: 283 us -> 246 us (0.87)
  waiting for transfers between devices: 106 us -> 164 us
  blocking collectives: 54.2 us -> 14.6 us
  local copies, waits for them, and re-layouts: 37 us -> 0.84 us
  other arithmetic: 15.4 us -> 4.04 us
  starting transfers between devices: 19.4 us -> 8.56 us
  matrix products: 35.7 us -> 39.6 us
    all_gather x0 -> x2, waiting for transfers between devices: none -> 75.6 us  [the longest x1 43.1 us: dispatch_gather(): all_dy = lax.all_gather(out_grad, 'expert', axis=0, tiled=False)]
    all_to_all x1 -> x0, blocking collectives: 54.2 us -> none  [shards(): lax.all_to_all(send_x, 'expert', split_axis=0, concat_axis=0, tiled=True)]
    all_to_all x2 -> x0, waiting for transfers between devices: 40.2 us -> none  [the longest x1 40.2 us: shards(): lax.all_to_all(send_dy, 'expert', split_axis=0, concat_axis=0, tiled=True)]
    gather x6 -> x0, local copies, waits for them, and re-layouts: 31.2 us -> none  [the longest x2 12.1 us: shards(): picked = back_x.reshape(experts * cap, width)[slot].astype(jnp.float32)]
    reduce_scatter x2, waiting for transfers between devices: 21.1 us -> 38.8 us  [the longest x1 38.8 us: shards(): lax.psum_scatter(grad_one, 'dp', scatter_dimension=0, tiled=True)]
    all_gather x0 -> x1, blocking collectives: none -> 14.6 us  [dispatch_gather(): table = lax.all_gather(table, 'expert', axis=0, tiled=False).astype(F32)]
    all_to_all x2 -> x0, starting transfers between devices: 10.7 us -> none  [the longest x1 6.35 us: shards(): lax.all_to_all(send_p, 'expert', split_axis=0, concat_axis=0, tiled=True)]
    select_n x4 -> x0, other arithmetic: 4.61 us -> none  [the longest x1 4.56 us: shards(): jnp.where(filled[:, None], tokens[source], zero_b)]
  transfers between devices with their start and end apart: 6 -> 6, of which waited for: 3 -> 4; matrix products, arithmetic and copies ran while one was open for 24% -> 12% of each run, Pallas kernels for 0% -> 0%
where the time goes in v1:
time: 246 us; the launch traced here: 245 us
  waiting for transfers between devices  164 us (67%)
  matrix products  39.6 us (16%)
  blocking collectives  14.6 us (6%)
  between operations  13.8 us (6%)
  starting transfers between devices  8.56 us (3%)
  other arithmetic  4.04 us (2%)
    all_to_all x1, waiting for transfers between devices, shards(): lax.all_to_all(row_grad.reshape(n_groups, cap, width), 'expert', split_ax...  48.1 us
    all_gather x1, waiting for transfers between devices, dispatch_gather(): all_dy = lax.all_gather(out_grad, 'expert', axis=0, tiled=False)  43.1 us
    reduce_scatter x1, waiting for transfers between devices, shards(): lax.psum_scatter(grad_one, 'dp', scatter_dimension=0, tiled=True)  38.8 us
    all_gather x1, waiting for transfers between devices, dispatch_gather(): all_x = lax.all_gather(tokens, 'expert', axis=0, tiled=False)  32.5 us
    all_gather x1, blocking collectives, dispatch_gather(): table = lax.all_gather(table, 'expert', axis=0, tiled=False).astype(F32)  14.6 us
    dot_general x1, matrix products, shards(): lax.dot_general(proj_grad, w_one, (((1,), (1,)), ((), ())), preferred_ele...  8.29 us
    dot_general x1, matrix products, shards(): lax.dot_general(rows_x, proj_grad, contract, preferred_element_type=F32)  8.13 us
    dot_general x2, matrix products, take(): lax.dot_general(pick, rows, (((2,), (1,)), ((0,), (0,))), preferred_eleme...  7.23 us
  transfers between devices with their start and end apart: 6, of which 4 were waited for; matrix products, arithmetic and copies ran while one was open for 12% of the time, Pallas kernels for 0%

profile of v1, /device:TPU:0, one launch (start us, length us, event | category | flops | bytes accessed | tf_op | source)
XLA Modules:
  0.0 245.4 jit_solution(123633695336855170)
XLA Ops:
  7.2 0.7 all-gather.9.cloned.1.call-update
  7.9 0.0 all-gather.7.cloned.1.call-start
  8.0 0.7 all-gather.7.cloned.1.call-update
  8.7 0.0 reduce-scatter.5.cloned.1.call-start
  8.7 0.7 fusion.25
  9.4 0.1 fusion.22
  9.5 0.7 select_reduce_fusion.2
  10.3 0.8 convert_bitcast_fusion
  11.0 0.7 maximum_bitcast_fusion
  11.7 14.6 %all-gather.3 = bf16[8,6,128]{2,1,0:T(8,128)(2,1)S(1)} all-gather(bf16[1,6,128]{2,1,0:T(8,128)(2,1)S(1)} %maximum_bitcast_fusion), channel_id=2, replica_groups=mesh['dp'=4,'expert'=8] {'expert'}, dimensions={0}, use_global_device_ids=true | all-gather | bytes 13824 | tf_op jit(solution)/shard_map/all_gather | solution.py:21
  26.3 0.1 fusion.23
  26.5 0.2 select_reduce_fusion.1
  26.6 0.1 mul.48
  26.7 32.5 %all-gather.9.cloned.1.call-done = bf16[1024,2048]{1,0:T(8,128)(2,1)} async-done(((bf16[128,2048]{1,0:T(8,128)(2,1)}), bf16[1024,2048]{1,0:T(8,128)(2,1)}) %all-gather.9.cloned.1.call-update) | async-done | bytes 4194320 | tf_op jit(solution)/shard_map/all_gather | solution.py:22
  59.2 4.2 %convolution_convert_fusion.2 = bf16[8,64,2048]{2,1,0:T(8,128)(2,1)} fusion(bf16[8,128,2048]{2,1,0:T(8,128)(2,1)} %bitcast.35, f32[8,128]{1,0:T(8,128)S(1)} %fusion.23, pred[8,128]{1,0:T(8,128)(4,1)S(1)} %reduce_or.29), kind=kOutput, calls=%fused_computation.9 | convolution fusion | flops 269615104 | bytes 6296576 | tf_op jit(solution)/shard_map/dot_general | solution.py:33
  63.4 43.1 %all-gather.7.cloned.1.call-done = bf16[1024,2048]{1,0:T(8,128)(2,1)} async-done(((bf16[128,2048]{1,0:T(8,128)(2,1)}), bf16[1024,2048]{1,0:T(8,128)(2,1)}) %all-gather.7.cloned.1.call-update) | async-done | bytes 4194320 | tf_op jit(solution)/shard_map/all_gather | solution.py:23
  106.5 3.0 %convolution_convert_fusion.3 = bf16[8,64,2048]{2,1,0:T(8,128)(2,1)S(1)} fusion(bf16[8,128,2048]{2,1,0:T(8,128)(2,1)} %bitcast.36, f32[8,128]{1,0:T(8,128)S(1)} %fusion.23, pred[8,128]{1,0:T(8,128)(4,1)S(1)} %reduce_or.29), kind=kOutput, calls=%fused_computation.10 | convolution fusion | flops 269615104 | bytes 6296576 | tf_op jit(solution)/shard_map/dot_general | solution.py:33
  109.6 5.5 %fusion.2 = f32[512,1536]{1,0:T(8,128)S(1)} fusion(bf16[512,2048]{1,0:T(8,128)(2,1)S(1)} %bitcast.38, bf16[1,2048,1536]{2,1,0:T(8,128)(2,1)} %param.10), kind=kOutput, calls=%fused_computation.3 | convolution fusion | flops 3221225472 | bytes 11534336 | tf_op jit(solution)/shard_map/dot_general | solution.py:85
  115.2 3.7 %fusion.9 = (bf16[512]{0:T(512)(128)(2,1)S(1)}, bf16[512,768]{1,0:T(8,128)(2,1)S(1)}, bf16[512,768]{1,0:T(8,128)(2,1)}, bf16[512,768]{1,0:T(8,128)(2,1)}) fusion(f32[512,1536]{1,0:T(8,128)S(1)} %fusion.2, f32[512]{0:T(512)S(1)} %mul.48, bf16[512,2048]{1,0:T(8,128)(2,1)S(1)} %bitcast.39, bf16[1,768,2048]{2,1,0:T(8,128)(2,1)S(1)} %copy-done), kind=kOutput, calls=%fused_computation.14 | convolution fusion | flops 1618083328 | bytes 10750976 | tf_op jit(solution)/shard_map/dot_general | solution.py:95
  118.8 3.7 %convolution_convert_fusion.1 = bf16[768,2048]{1,0:T(8,128)(2,1)} fusion(bf16[512,2048]{1,0:T(8,128)(2,1)S(1)} %bitcast.40, bf16[512,768]{1,0:T(8,128)(2,1)S(1)} %get-tuple-element.5, f32[512]{0:T(512)S(1)} %mul.48), kind=kOutput, calls=%fused_computation.5 | convolution fusion | flops 1613365248 | bytes 6031360 | tf_op jit(solution)/shard_map/dot_general | solution.py:92
  122.5 0.0 reduce-scatter.3.cloned.1.call-start
  122.6 8.1 %convolution_convert_fusion = bf16[2048,1536]{1,0:T(8,128)(2,1)} fusion(bf16[512,2048]{1,0:T(8,128)(2,1)} %bitcast.37, bf16[512,768]{1,0:T(8,128)(2,1)} %get-tuple-element.10, bf16[512,768]{1,0:T(8,128)(2,1)} %get-tuple-element.11), kind=kOutput, calls=%fused_computation | convolution fusion | flops 3227516928 | bytes 9961472 | tf_op jit(solution)/shard_map/dot_general | solution.py:101
  130.7 0.7 convert_element_type.95
  131.4 3.5 %all-to-all-start.1 = ((bf16[8,1,64]{2,1,0:T(2,128)(2,1)}), bf16[8,1,64]{2,1,0:T(2,128)(2,1)S(1)}, u32[]{:S(2)}, u32[]{:S(2)}) async-start(bf16[8,1,64]{2,1,0:T(2,128)(2,1)} %convert_element_type.95), calls=%async_computation.1 | async-start | bytes 8192 | tf_op jit(solution)/shard_map/all_to_all | solution.py:110
  134.9 8.3 %fusion.6 = bf16[512,2048]{1,0:T(8,128)(2,1)} fusion(bf16[1,2048,1536]{2,1,0:T(8,128)(2,1)} %param.10, bf16[512,768]{1,0:T(8,128)(2,1)} %get-tuple-element.10, bf16[512,768]{1,0:T(8,128)(2,1)} %get-tuple-element.11), kind=kOutput, calls=%fused_computation.8 | convolution fusion | flops 3225419776 | bytes 9961472 | tf_op jit(solution)/shard_map/dot_general | solution.py:104
  143.2 4.9 %all-to-all-start = ((bf16[8,64,2048]{2,1,0:T(8,128)(2,1)}), bf16[8,64,2048]{2,1,0:T(8,128)(2,1)}, u32[]{:S(2)}, u32[]{:S(2)}) async-start(bf16[8,64,2048]{2,1,0:T(8,128)(2,1)} %bitcast.41), calls=%async_computation | async-start | bytes 4194304 | tf_op jit(solution)/shard_map/all_to_all | solution.py:107
  148.1 0.2 fusion.14
  148.3 0.1 reshape.50
  148.4 0.8 select_reduce_fusion
  149.2 48.1 %all-to-all-done = bf16[8,64,2048]{2,1,0:T(8,128)(2,1)} async-done(((bf16[8,64,2048]{2,1,0:T(8,128)(2,1)}), bf16[8,64,2048]{2,1,0:T(8,128)(2,1)}, u32[]{:S(2)}, u32[]{:S(2)}) %all-to-all-start) | async-done | bytes 2097184 | tf_op jit(solution)/shard_map/all_to_all | solution.py:107
  197.3 2.8 %convolution_convert_fusion.4 = bf16[128,2048]{1,0:T(8,128)(2,1)} fusion(pred[128,512]{1,0:T(8,128)(4,1)S(1)} %fusion.14, bf16[512,2048]{1,0:T(8,128)(2,1)} %bitcast.10), kind=kOutput, calls=%fused_computation.11 | convolution fusion | flops 268697600 | bytes 2686976 | tf_op jit(solution)/shard_map/dot_general | solution.py:116
  200.1 38.8 %reduce-scatter.3.cloned.1.call-done = bf16[512,1536]{1,0:T(8,128)(2,1)} async-done(((bf16[2048,1536]{1,0:T(8,128)(2,1)}), bf16[512,1536]{1,0:T(8,128)(2,1)}) %reduce-scatter.3.cloned.1.call-update) | async-done | bytes 1572880 | tf_op jit(solution)/shard_map/reduce_scatter | solution.py:102
  (13 shorter events, 0.2 us)
Async XLA Ops:
  7.2 108.0 %copy-start = (bf16[1,768,2048]{2,1,0:T(8,128)(2,1)S(1)}, bf16[1,768,2048]{2,1,0:T(8,128)(2,1)}, u32[]{:S(2)}) copy-start(bf16[1,768,2048]{2,1,0:T(8,128)(2,1)} %param.11) | copy-start | bytes 9437188
  7.2 52.1 %all-gather.9.cloned.1.call-start = ((), (), s32[]{:S(2)}) async-start(), calls=%async_computation.7 | async-start | bytes 4718592 | tf_op jit(solution)/shard_map/all_gather | solution.py:22
  7.9 98.6 %all-gather.7.cloned.1.call-start = ((), (), s32[]{:S(2)}) async-start(), calls=%async_computation.6 | async-start | bytes 4718592 | tf_op jit(solution)/shard_map/all_gather | solution.py:23
  8.7 191.4 %reduce-scatter.5.cloned.1.call-start = ((), (), s32[]{:S(2)}) async-start(), calls=%async_computation.5 | async-start | bytes 3932160 | tf_op jit(solution)/shard_map/reduce_scatter | solution.py:93
  106.5 3.0 %copy-start.1 = (bf16[8,64,2048]{2,1,0:T(8,128)(2,1)S(1)}, bf16[8,64,2048]{2,1,0:T(8,128)(2,1)}, u32[]{:S(2)}) copy-start(bf16[8,64,2048]{2,1,0:T(8,128)(2,1)} %convolution_convert_fusion.2) | copy-start | bytes 6291460
  122.5 116.3 %reduce-scatter.3.cloned.1.call-start = ((), (), s32[]{:S(2)}) async-start(), calls=%async_computation.4 | async-start | bytes 7864320 | tf_op jit(solution)/shard_map/reduce_scatter | solution.py:102
  131.4 11.8 %all-to-all-start.1 = ((bf16[8,1,64]{2,1,0:T(2,128)(2,1)}), bf16[8,1,64]{2,1,0:T(2,128)(2,1)S(1)}, u32[]{:S(2)}, u32[]{:S(2)}) async-start(bf16[8,1,64]{2,1,0:T(2,128)(2,1)} %convert_element_type.95), calls=%async_computation.1 | async-start | bytes 8192 | tf_op jit(solution)/shard_map/all_to_all | solution.py:110
  143.2 54.0 %all-to-all-start = ((bf16[8,64,2048]{2,1,0:T(8,128)(2,1)}), bf16[8,64,2048]{2,1,0:T(8,128)(2,1)}, u32[]{:S(2)}, u32[]{:S(2)}) async-start(bf16[8,64,2048]{2,1,0:T(8,128)(2,1)} %bitcast.41), calls=%async_computation | async-start | bytes 4194304 | tf_op jit(solution)/shard_map/all_to_all | solution.py:107
Sparse Core Ops, SparseCore 0:
  9.6 49.6 all-gather.8
  60.8 45.6 all-gather.6
  122.7 42.7 reduce-scatter.4
  168.8 70.0 reduce-scatter.2
